TPU v7x, 256 devices: a whole 4x4x8 slice. The times are simulated.
256 devices in a mesh: blk: 64 (over z, x, core), ch: 4 (over y).
Axes of the slice: x: 4, y: 4, z: 8, core: 2. Of those that a mesh axis runs over, the one named last changes fastest.
Arguments:
- features: bfloat16 [128, 65536], P('ch', 'blk'), may hold values from -6 to 6
- weight: bfloat16 [27, 128, 128], P(None, 'ch'), may hold values from -0.1875 to 0.1875
- grad_out: bfloat16 [128, 65536], P('ch', 'blk'), may hold values from -6 to 6
- rulebook: int32 [27, 65536], P(None, 'blk'), may hold values from 0 to 1280, as said below
Outputs:
- output: bfloat16 [128, 65536], P('ch', 'blk')
- grad_features: bfloat16 [128, 65536], P('ch', 'blk')
- weight_grad: float32 [27, 128, 128], P(None, 'ch')
Inputs may be any that keep to these rules, and one draw needn't show every extreme that they name: `rulebook`: slots 0 to 127 of every block hold active voxels of its lowest layer, slots 128 to 255 active voxels of its highest layer, then come active inner voxels, then empty slots; at least 640 slots of a block are active and some block has all 1024. Offset k = 9 (dx + 1) + 3 (dy + 1) + (dz + 1), dz along the block order. An entry names the table column of the active neighbour at that offset, and the zero column 1280 for an inactive neighbour, one outside the image, and for every entry of an empty slot. If entry k of slot i names slot j, entry 26 - k of j names i.
All inputs are finite; a program needn't handle non-finite values.
Results may differ from a plain program's by a relative error of at most 0.001.
Values may be sent and summed in bfloat16 or wider, within the bound.
No kernel may reach another device: no remote copies, remote signals or barrier semaphores. Data moves between devices by JAX's collectives and lax.ppermute only.
A program may use at most 64 MiB of HBM per device.

v0:
```python
import math
import jax
import jax.numpy as jnp
from jax import lax
from jax.sharding import PartitionSpec as P

VOX = 1024
FACE = 128


def passed_along(value, axis, steps):
    count = lax.axis_size(axis)
    pairs = [(source, (source + steps) % count) for source in range(count)]
    return lax.ppermute(value, axis, pairs)


def split_faces(source):
    chan_count = source.shape[0]
    blocks = source.reshape(chan_count, source.shape[1] // VOX, VOX)
    lowest = blocks[:, :, :FACE].reshape(chan_count, -1)
    highest = blocks[:, :, FACE : 2 * FACE].reshape(chan_count, -1)
    return (lowest, highest)


def align(from_lower, from_upper):
    chan_count = from_lower.shape[0]
    lower_faces = from_lower.reshape(chan_count, -1, FACE)
    upper_faces = from_upper.reshape(chan_count, -1, FACE)
    blank_faces = jnp.zeros_like(lower_faces)
    position = lax.axis_index("blk")
    final_index = lax.axis_size("blk") - 1
    lower_faces = jnp.where(
        position == 0, jnp.concatenate([blank_faces, lower_faces[:, :-1]], axis=1), lower_faces
    )
    upper_faces = jnp.where(
        position == final_index,
        jnp.concatenate([upper_faces[:, 1:], blank_faces], axis=1),
        upper_faces,
    )
    return (lower_faces.reshape(chan_count, -1), upper_faces.reshape(chan_count, -1))


def extend(source, lower_faces, upper_faces):
    zero_column = jnp.zeros((source.shape[0], 1), source.dtype)
    return jnp.concatenate([source, lower_faces, upper_faces, zero_column], axis=1)


def densify(table, neighbours):
    table_rows = table.T
    picked_rows = jnp.take(table_rows, neighbours, axis=0)
    return picked_rows.reshape(neighbours.shape[0], -1)


def per_device(features, weight, grad_out, rulebook):
    quarter = features.shape[0]
    local_rows = features.shape[1]
    width = weight.shape[2]
    neighbours = rulebook.T
    lowest, highest = split_faces(features)
    from_lower = passed_along(highest, "blk", 1)
    from_upper = passed_along(lowest, "blk", -1)
    lower_faces, upper_faces = align(from_lower, from_upper)
    ext_inputs = extend(features, lower_faces, upper_faces)
    dense_inputs = densify(ext_inputs, neighbours)
    flat_weight = weight.reshape(27 * quarter, width)
    output = lax.psum_scatter(
        jnp.dot(dense_inputs, flat_weight, preferred_element_type=jnp.float32).T,
        "ch",
        scatter_dimension=0,
        tiled=True,
    )
    output = output.astype(jnp.bfloat16)
    grad_full = lax.all_gather(grad_out, "ch", axis=0, tiled=True)
    grad_lowest, grad_highest = split_faces(grad_full)
    grad_lower = passed_along(grad_highest, "blk", 1)
    grad_upper = passed_along(grad_lowest, "blk", -1)
    lower_grads, upper_grads = align(grad_lower, grad_upper)
    ext_grads = extend(grad_full, lower_grads, upper_grads)
    flipped = neighbours[:, ::-1]
    dense_grads = densify(ext_grads, flipped)
    back_weight = weight.transpose(0, 2, 1).reshape(27 * width, quarter)
    grad_inputs = jnp.dot(dense_grads, back_weight, preferred_element_type=jnp.float32).T
    local_terms = lax.dot_general(
        dense_inputs, grad_full.T, (((0,), (0,)), ((), ())), preferred_element_type=jnp.float32
    )
    local_terms = local_terms.reshape(27, quarter, width)
    norm_scale = 1.0 / math.sqrt(lax.axis_size("blk") * local_rows)
    weight_grad = lax.psum(local_terms, "blk") * norm_scale
    return (output, grad_inputs.astype(jnp.bfloat16), weight_grad)


def solution(mesh):
    placed = (P("ch", "blk"), P(None, "ch", None), P("ch", "blk"), P(None, "blk"))
    return jax.shard_map(
        per_device,
        mesh=mesh,
        in_specs=placed,
        out_specs=(P("ch", "blk"), P("ch", "blk"), P(None, "ch", None)),
        check_vma=False,
    )
```

profile of v0, /device:TPU:1, one launch (start us, length us, event | category | flops | bytes accessed | tf_op | source)
XLA Modules:
  0.0 368.4 jit_solution(6934085552225605736)
XLA Ops:
  8.1 11.6 %all_gather.3 = bf16[128,1024]{1,0:T(8,128)(2,1)S(1)} all-gather(bf16[32,1024]{1,0:T(8,128)(2,1)} %param.6), channel_id=1, replica_groups=mesh['blk'=64,'ch'=4] {'ch'}, dimensions={0}, use_global_device_ids=true | all-gather | bytes 327680 | tf_op jit(solution)/shard_map/all_gather | solution.py:73
  19.7 4.7 %collective-permute-start.3 = (bf16[128,128]{1,0:T(8,128)(2,1)S(1)}, bf16[128,128]{1,0:T(8,128)(2,1)S(1)}, u32[]{:S(2)}, u32[]{:S(2)}) collective-permute-start(bf16[128,128]{1,0:T(8,128)(2,1)S(1)} %get-tuple-element.16), channel_id=1, source_target_pairs={{0,252},{4,0},{8,4},{12,8},{16,12},{20,16},{24,20},{28,24},{32,28}... | collective-permute-start | bytes 98312 | tf_op jit(solution)/shard_map/ppermute | solution.py:14
  24.3 0.7 slice_bitcast_fusion.3
  25.0 3.6 collective-permute-start.1
  28.6 2.9 rev.3
  31.6 0.9 compare_select_fusion.1
  33.8 0.9 compare_and_fusion.1
  35.4 0.9 maximum_maximum_fusion
  36.5 96.4 %gather_fusion = bf16[27648,32]{1,0:T(8,128)(2,1)} fusion(bf16[1281,32]{1,0:T(8,128)(2,1)S(1)} %bitcast.48, s32[27648]{0:T(1024)S(1)} %broadcast_clamp_fusion.1), kind=kCustom, calls=%fused_computation | custom fusion | bytes 3649536 | tf_op jit(solution)/shard_map/jit(_take)/gather | solution.py:50
  132.9 5.4 %copy.40 = bf16[27648,32]{0,1:T(8,128)(2,1)S(1)} copy(bf16[27648,32]{1,0:T(8,128)(2,1)} %gather_fusion) | data formatting | bytes 3538944 | tf_op jit(solution)/shard_map/jit(_take)/gather | solution.py:50
  138.3 22.7 %reshape.67 = bf16[1024,27,32]{1,0,2:T(8,128)(2,1)} reshape(bf16[27648,32]{0,1:T(8,128)(2,1)S(1)} %copy.40) | data formatting | bytes 3538944 | tf_op jit(solution)/shard_map/jit(_take)/gather | solution.py:50
  161.0 7.7 %broadcast_select_fusion.1 = bf16[1024,27,32]{1,0,2:T(8,128)(2,1)} fusion(bf16[1024,27,32]{1,0,2:T(8,128)(2,1)} %reshape.67, pred[1024,27]{1,0:T(8,128)(4,1)S(1)} %copy.37), kind=kLoop, calls=%fused_computation.3 | loop fusion | flops 884736 | bytes 3566592 | tf_op jit(solution)/shard_map/jit(_take)/select_n | solution.py:50
  168.7 7.5 %copy.47 = bf16[1024,27,32]{0,2,1:T(8,128)(2,1)S(1)} copy(bf16[1024,27,32]{1,0,2:T(8,128)(2,1)} %broadcast_select_fusion.1) | data formatting | bytes 3538944 | tf_op jit(solution)/shard_map/jit(_take)/select_n | solution.py:50
  176.3 1.4 fusion.2
  177.9 5.1 %convolution_bitcast_fusion = f32[128,1024]{0,1:T(8,128)S(1)} fusion(bf16[1024,27,32]{1,0,2:T(8,128)(2,1)} %broadcast_select_fusion.1, bf16[27,32,128]{2,1,0:T(8,128)(2,1)S(1)} %copy-done), kind=kOutput, calls=%fused_computation.8 | convolution fusion | flops 226492416 | bytes 2514944 | tf_op jit(solution)/shard_map/dot_general | solution.py:67
  183.1 1.0 copy.50
  184.4 96.4 %gather_fusion.1 = bf16[27648,128]{1,0:T(8,128)(2,1)} fusion(bf16[1281,128]{1,0:T(8,128)(2,1)S(1)} %copy.45, s32[27648]{0:T(1024)S(1)} %broadcast_clamp_fusion), kind=kCustom, calls=%fused_computation.1 | custom fusion | bytes 14266368 | tf_op jit(solution)/shard_map/jit(_take)/gather | solution.py:50
  280.8 11.9 %reshape.75 = bf16[1024,27,128]{2,1,0:T(8,128)(2,1)} reshape(bf16[27648,128]{1,0:T(8,128)(2,1)} %gather_fusion.1) | data formatting | bytes 14155776 | tf_op jit(solution)/shard_map/jit(_take)/gather | solution.py:50
  292.7 15.3 %broadcast_select_fusion = bf16[1024,27,128]{2,1,0:T(8,128)(2,1)S(1)} fusion(bf16[1024,27,128]{2,1,0:T(8,128)(2,1)} %reshape.75, pred[1024,27]{1,0:T(8,128)(4,1)S(1)} %copy.43), kind=kLoop, calls=%fused_computation.2 | loop fusion | flops 3538944 | bytes 14183424 | tf_op jit(solution)/shard_map/jit(_take)/select_n | solution.py:50
  308.1 4.3 %fusion.10 = bf16[32,1024]{1,0:T(8,128)(2,1)} fusion(bf16[1024,27,128]{2,1,0:T(8,128)(2,1)S(1)} %broadcast_select_fusion, bf16[27,32,128]{2,1,0:T(8,128)(2,1)S(1)} %copy-done), kind=kOutput, calls=%fused_computation.11 | convolution fusion | flops 226525184 | bytes 7364608 | tf_op jit(solution)/shard_map/dot_general | solution.py:82
  312.4 44.9 %all-reduce.2.cloned.1.call-done = f32[27,32,128]{2,1,0:T(8,128)} async-done(((f32[27,32,128]{2,1,0:T(8,128)}), f32[27,32,128]{2,1,0:T(8,128)}) %all-reduce.2.cloned.1.call-update) | async-done | bytes 442384 | tf_op jit(solution)/shard_map/psum | solution.py:88
  357.3 1.8 broadcast_multiply_fusion
  359.1 1.1 copy.51
  360.2 0.8 copy.48
  (32 shorter events, 2.7 us)
Async XLA Ops:
  8.0 169.9 %copy-start = (bf16[27,32,128]{2,1,0:T(8,128)(2,1)S(1)}, bf16[27,32,128]{2,1,0:T(8,128)(2,1)}, u32[]{:S(2)}) copy-start(bf16[27,32,128]{2,1,0:T(8,128)(2,1)} %param.5) | copy-start | bytes 663556
  8.0 349.3 %all-reduce.2.cloned.1.call-start = ((), (), s32[]{:S(2)}) async-start(), calls=%async_computation.1 | async-start | bytes 884736 | tf_op jit(solution)/shard_map/psum | solution.py:88
  19.7 164.4 %collective-permute-start.3 = (bf16[128,128]{1,0:T(8,128)(2,1)S(1)}, bf16[128,128]{1,0:T(8,128)(2,1)S(1)}, u32[]{:S(2)}, u32[]{:S(2)}) collective-permute-start(bf16[128,128]{1,0:T(8,128)(2,1)S(1)} %get-tuple-element.16), channel_id=1, source_target_pairs={{0,252},{4,0},{8,4},{12,8},{16,12},{20,16},{24,20},{28,24},{32,28}... | collective-permute-start | bytes 98312 | tf_op jit(solution)/shard_map/ppermute | solution.py:14
  24.3 159.8 %collective-permute-start.2 = (bf16[128,128]{1,0:T(8,128)(2,1)S(1)}, bf16[128,128]{1,0:T(8,128)(2,1)S(1)}, u32[]{:S(2)}, u32[]{:S(2)}) collective-permute-start(bf16[128,128]{1,0:T(8,128)(2,1)S(1)} %get-tuple-element.15), channel_id=1, source_target_pairs={{0,4},{4,8},{8,12},{12,16},{16,20},{20,24},{24,28},{28,32},{32,36}... | collective-permute-start | bytes 98312 | tf_op jit(solution)/shard_map/ppermute | solution.py:14
  25.0 10.3 %collective-permute-start.1 = (bf16[32,128]{1,0:T(8,128)(2,1)S(1)}, bf16[32,128]{1,0:T(8,128)(2,1)S(1)}, u32[]{:S(2)}, u32[]{:S(2)}) collective-permute-start(bf16[32,128]{1,0:T(8,128)(2,1)S(1)} %get-tuple-element.18), channel_id=1, source_target_pairs={{0,252},{4,0},{8,4},{12,8},{16,12},{20,16},{24,20},{28,24},{32,28}... | collective-permute-start | bytes 24584 | tf_op jit(solution)/shard_map/ppermute | solution.py:14
  28.6 6.7 %collective-permute-start = (bf16[32,128]{1,0:T(8,128)(2,1)S(1)}, bf16[32,128]{1,0:T(8,128)(2,1)S(1)}, u32[]{:S(2)}, u32[]{:S(2)}) collective-permute-start(bf16[32,128]{1,0:T(8,128)(2,1)S(1)} %get-tuple-element.17), channel_id=1, source_target_pairs={{0,4},{4,8},{8,12},{12,16},{16,20},{20,24},{24,28},{28,32},{32,36}... | collective-permute-start | bytes 24584 | tf_op jit(solution)/shard_map/ppermute | solution.py:14
  177.7 181.4 %reduce-scatter.4.cloned.1.call-start = ((), (), s32[]{:S(2)}) async-start(), calls=%async_computation.2 | async-start | bytes 655360
Sparse Core Ops, SparseCore 0:
  177.8 179.4 all-reduce.1
Sparse Core Ops, SparseCore 1:
  184.2 23.4 reduce-scatter.3
where the time goes:
time: 370 us; the launch traced here: 368 us
  local copies, waits for them, and re-layouts  249 us (67%)
  waiting for transfers between devices  44.9 us (12%)
  other arithmetic  27.8 us (8%)
  between operations  15.7 us (4%)
  blocking collectives  11.6 us (3%)
  matrix products  10.9 us (3%)
  starting transfers between devices  8.51 us (2%)
    gather x5, local copies, waits for them, and re-layouts, densify(): picked_rows = jnp.take(table_rows, neighbours, axis=0)  233 us
    psum x1, waiting for transfers between devices, per_device(): weight_grad = lax.psum(local_terms, 'blk') * norm_scale  44.9 us
    select_n x4, other arithmetic, densify(): picked_rows = jnp.take(table_rows, neighbours, axis=0)  24 us
    all_gather x1, blocking collectives, per_device(): grad_full = lax.all_gather(grad_out, 'ch', axis=0, tiled=True)  11.6 us
    ppermute x4, starting transfers between devices, passed_along(): return lax.ppermute(value, axis, pairs)  8.25 us
    select_n x3, local copies, waits for them, and re-layouts, densify(): picked_rows = jnp.take(table_rows, neighbours, axis=0)  7.95 us
  transfers between devices with their start and end apart: 6, of which 1 were waited for; matrix products, arithmetic and copies ran while one was open for 78% of the time, Pallas kernels for 0%

commit v1 on v0

--- a/solution.py
+++ b/solution.py
@@ -85,7 +85,7 @@
     )
     local_terms = local_terms.reshape(27, quarter, width)
     norm_scale = 1.0 / math.sqrt(lax.axis_size("blk") * local_rows)
-    weight_grad = lax.psum(local_terms, "blk") * norm_scale
+    weight_grad = jnp.sum(lax.all_gather(local_terms, "blk"), axis=0) * norm_scale
     return (output, grad_inputs.astype(jnp.bfloat16), weight_grad)
 
 

time: 370 us -> 341 us (0.922)
  waiting for transfers between devices: 44.9 us -> 3.65 us
  other arithmetic: 27.8 us -> 37.2 us
  starting transfers between devices: 8.51 us -> 12.5 us
    psum x1 -> x0, waiting for transfers between devices: 44.9 us -> none  [per_device(): weight_grad = lax.psum(local_terms, 'blk') * norm_scale]
    reduce_sum x0 -> x1, other arithmetic: none -> 10.4 us  [per_device(): jnp.sum(lax.all_gather(local_terms, 'blk'), axis=0) * norm_scale]
    ppermute x4, starting transfers between devices: 8.25 us -> 12.4 us  [passed_along(): return lax.ppermute(value, axis, pairs)]
  transfers between devices with their start and end apart: 6 -> 6, of which waited for: 1 -> 1; matrix products, arithmetic and copies ran while one was open for 78% -> 43% of each run, Pallas kernels for 0% -> 0%
where the time goes in v1:
time: 341 us; the launch traced here: 336 us
  local copies, waits for them, and re-layouts  246 us (72%)
  other arithmetic  37.2 us (11%)
  between operations  15.7 us (5%)
  starting transfers between devices  12.5 us (4%)
  matrix products  10.9 us (3%)
  blocking collectives  9.89 us (3%)
  waiting for transfers between devices  3.65 us (1%)
    gather x5, local copies, waits for them, and re-layouts, densify(): picked_rows = jnp.take(table_rows, neighbours, axis=0)  233 us
    select_n x4, other arithmetic, densify(): picked_rows = jnp.take(table_rows, neighbours, axis=0)  24 us
    ppermute x4, starting transfers between devices, passed_along(): return lax.ppermute(value, axis, pairs)  12.4 us
    reduce_sum x1, other arithmetic, per_device(): jnp.sum(lax.all_gather(local_terms, 'blk'), axis=0) * norm_scale  10.4 us
    all_gather x1, blocking collectives, per_device(): grad_full = lax.all_gather(grad_out, 'ch', axis=0, tiled=True)  9.89 us
    select_n x3, local copies, waits for them, and re-layouts, densify(): picked_rows = jnp.take(table_rows, neighbours, axis=0)  7.96 us
  transfers between devices with their start and end apart: 6, of which 1 were waited for; matrix products, arithmetic and copies ran while one was open for 43% of the time, Pallas kernels for 0%

profile of v1, /device:TPU:1, one launch (start us, length us, event | category | flops | bytes accessed | tf_op | source)
XLA Modules:
  0.0 336.2 jit_solution(4780977653362426986)
XLA Ops:
  8.1 0.8 slice_bitcast_fusion.3
  8.8 3.2 collective-permute-start.1
  12.1 0.9 compare_select_fusion.1
  13.6 0.9 compare_and_fusion.1
  14.9 3.6 %collective-permute-done = bf16[32,128]{1,0:T(8,128)(2,1)S(1)} collective-permute-done((bf16[32,128]{1,0:T(8,128)(2,1)S(1)}, bf16[32,128]{1,0:T(8,128)(2,1)S(1)}, u32[]{:S(2)}, u32[]{:S(2)}) %collective-permute-start) | collective-permute-done | bytes 8224 | tf_op jit(solution)/shard_map/ppermute | solution.py:14
  18.5 0.9 maximum_maximum_fusion
  19.6 96.4 %gather_fusion = bf16[27648,32]{1,0:T(8,128)(2,1)} fusion(bf16[1281,32]{1,0:T(8,128)(2,1)S(1)} %bitcast.49, s32[27648]{0:T(1024)S(1)} %broadcast_clamp_fusion.1), kind=kCustom, calls=%fused_computation | custom fusion | bytes 3649536 | tf_op jit(solution)/shard_map/jit(_take)/gather | solution.py:50
  116.0 5.4 %copy.40 = bf16[27648,32]{0,1:T(8,128)(2,1)S(1)} copy(bf16[27648,32]{1,0:T(8,128)(2,1)} %gather_fusion) | data formatting | bytes 3538944 | tf_op jit(solution)/shard_map/jit(_take)/gather | solution.py:50
  121.4 22.7 %reshape.72 = bf16[1024,27,32]{1,0,2:T(8,128)(2,1)} reshape(bf16[27648,32]{0,1:T(8,128)(2,1)S(1)} %copy.40) | data formatting | bytes 3538944 | tf_op jit(solution)/shard_map/jit(_take)/gather | solution.py:50
  144.1 7.7 %broadcast_select_fusion.1 = bf16[1024,27,32]{1,0,2:T(8,128)(2,1)} fusion(bf16[1024,27,32]{1,0,2:T(8,128)(2,1)} %reshape.72, pred[1024,27]{1,0:T(8,128)(4,1)S(1)} %copy.37), kind=kLoop, calls=%fused_computation.3 | loop fusion | flops 884736 | bytes 3566592 | tf_op jit(solution)/shard_map/jit(_take)/select_n | solution.py:50
  151.8 5.2 %convolution_bitcast_fusion = f32[128,1024]{0,1:T(8,128)S(1)} fusion(bf16[1024,27,32]{1,0,2:T(8,128)(2,1)} %broadcast_select_fusion.1, bf16[27,32,128]{2,1,0:T(8,128)(2,1)S(1)} %copy-done), kind=kOutput, calls=%fused_computation.8 | convolution fusion | flops 226492416 | bytes 2514944 | tf_op jit(solution)/shard_map/dot_general | solution.py:67
  157.0 1.0 copy.50
  158.1 9.9 %all_gather.6 = bf16[128,1024]{1,0:T(8,128)(2,1)S(1)} all-gather(bf16[32,1024]{1,0:T(8,128)(2,1)S(1)} %copy-done.2), channel_id=1, replica_groups=mesh['blk'=64,'ch'=4] {'ch'}, dimensions={0}, use_global_device_ids=true | all-gather | bytes 327680 | tf_op jit(solution)/shard_map/all_gather | solution.py:73
  167.9 7.5 %copy.47 = bf16[1024,27,32]{0,2,1:T(8,128)(2,1)S(1)} copy(bf16[1024,27,32]{1,0,2:T(8,128)(2,1)} %broadcast_select_fusion.1) | data formatting | bytes 3538944 | tf_op jit(solution)/shard_map/jit(_take)/select_n | solution.py:50
  175.5 1.4 fusion.2
  176.9 9.2 %collective-permute-start.3 = (bf16[128,128]{1,0:T(8,128)(2,1)S(1)}, bf16[128,128]{1,0:T(8,128)(2,1)S(1)}, u32[]{:S(2)}, u32[]{:S(2)}) collective-permute-start(bf16[128,128]{1,0:T(8,128)(2,1)S(1)} %get-tuple-element.16), channel_id=1, source_target_pairs={{0,252},{4,0},{8,4},{12,8},{16,12},{20,16},{24,20},{28,24},{32,28}... | collective-permute-start | bytes 98312 | tf_op jit(solution)/shard_map/ppermute | solution.py:14
  187.6 96.4 %gather_fusion.1 = bf16[27648,128]{1,0:T(8,128)(2,1)} fusion(bf16[1281,128]{1,0:T(8,128)(2,1)S(1)} %copy.45, s32[27648]{0:T(1024)S(1)} %broadcast_clamp_fusion), kind=kCustom, calls=%fused_computation.1 | custom fusion | bytes 14266368 | tf_op jit(solution)/shard_map/jit(_take)/gather | solution.py:50
  284.0 12.0 %reshape.80 = bf16[1024,27,128]{2,1,0:T(8,128)(2,1)} reshape(bf16[27648,128]{1,0:T(8,128)(2,1)} %gather_fusion.1) | data formatting | bytes 14155776 | tf_op jit(solution)/shard_map/jit(_take)/gather | solution.py:50
  296.1 15.4 %broadcast_select_fusion = bf16[1024,27,128]{2,1,0:T(8,128)(2,1)S(1)} fusion(bf16[1024,27,128]{2,1,0:T(8,128)(2,1)} %reshape.80, pred[1024,27]{1,0:T(8,128)(4,1)S(1)} %copy.43), kind=kLoop, calls=%fused_computation.2 | loop fusion | flops 3538944 | bytes 14183424 | tf_op jit(solution)/shard_map/jit(_take)/select_n | solution.py:50
  311.4 4.3 %fusion.10 = bf16[32,1024]{1,0:T(8,128)(2,1)} fusion(bf16[1024,27,128]{2,1,0:T(8,128)(2,1)S(1)} %broadcast_select_fusion, bf16[27,32,128]{2,1,0:T(8,128)(2,1)S(1)} %copy-done), kind=kOutput, calls=%fused_computation.11 | convolution fusion | flops 226525184 | bytes 7364608 | tf_op jit(solution)/shard_map/dot_general | solution.py:82
  315.7 1.1 copy.51
  316.8 0.8 copy.48
  317.6 10.4 %reduce_sum.9 = f32[27,32,128]{2,1,0:T(8,128)S(1)} reduce(f32[64,27,32,128]{3,2,1,0:T(8,128)} %bitcast.50, f32[]{:T(128)} %constant.44.clone.1), dimensions={0}, to_apply=%region_1.2 | reduce | flops 6967296 | bytes 28753924 | tf_op jit(solution)/shard_map/reduce_sum | solution.py:88
  328.0 0.8 broadcast_multiply_fusion
  (37 shorter events, 2.7 us)
Async XLA Ops:
  8.0 143.8 %copy-start = (bf16[27,32,128]{2,1,0:T(8,128)(2,1)S(1)}, bf16[27,32,128]{2,1,0:T(8,128)(2,1)}, u32[]{:S(2)}) copy-start(bf16[27,32,128]{2,1,0:T(8,128)(2,1)} %param.5) | copy-start | bytes 663556
  8.0 307.7 %reduce-scatter.4.cloned.1.call-start = ((), (), s32[]{:S(2)}) async-start(), calls=%async_computation.2 | async-start | bytes 655360
  8.8 6.0 %collective-permute-start.1 = (bf16[32,128]{1,0:T(8,128)(2,1)S(1)}, bf16[32,128]{1,0:T(8,128)(2,1)S(1)}, u32[]{:S(2)}, u32[]{:S(2)}) collective-permute-start(bf16[32,128]{1,0:T(8,128)(2,1)S(1)} %get-tuple-element.18), channel_id=1, source_target_pairs={{0,252},{4,0},{8,4},{12,8},{16,12},{20,16},{24,20},{28,24},{32,28}... | collective-permute-start | bytes 24584 | tf_op jit(solution)/shard_map/ppermute | solution.py:14
  12.1 6.4 %collective-permute-start = (bf16[32,128]{1,0:T(8,128)(2,1)S(1)}, bf16[32,128]{1,0:T(8,128)(2,1)S(1)}, u32[]{:S(2)}, u32[]{:S(2)}) collective-permute-start(bf16[32,128]{1,0:T(8,128)(2,1)S(1)} %get-tuple-element.17), channel_id=1, source_target_pairs={{0,4},{4,8},{8,12},{12,16},{16,20},{20,24},{24,28},{28,32},{32,36}... | collective-permute-start | bytes 24584 | tf_op jit(solution)/shard_map/ppermute | solution.py:14
  151.8 6.3 %copy-start.2 = (bf16[32,1024]{1,0:T(8,128)(2,1)S(1)}, bf16[32,1024]{1,0:T(8,128)(2,1)}, u32[]{:S(2)}) copy-start(bf16[32,1024]{1,0:T(8,128)(2,1)} %param.6) | copy-start | bytes 196612
  157.0 29.1 %copy-start.1 = (s32[27,1024]{1,0:T(8,128)S(1)}, s32[27,1024]{1,0:T(8,128)}, u32[]{:S(2)}) copy-start(s32[27,1024]{1,0:T(8,128)} %param.7) | copy-start | bytes 331780
  158.0 159.6 %all-gather.3.cloned.1.call-start = ((), (), s32[]{:S(2)}) async-start(), calls=%async_computation.1 | async-start | bytes 28753920 | tf_op jit(solution)/shard_map/all_gather | solution.py:88
  176.9 10.4 %collective-permute-start.3 = (bf16[128,128]{1,0:T(8,128)(2,1)S(1)}, bf16[128,128]{1,0:T(8,128)(2,1)S(1)}, u32[]{:S(2)}, u32[]{:S(2)}) collective-permute-start(bf16[128,128]{1,0:T(8,128)(2,1)S(1)} %get-tuple-element.16), channel_id=1, source_target_pairs={{0,252},{4,0},{8,4},{12,8},{16,12},{20,16},{24,20},{28,24},{32,28}... | collective-permute-start | bytes 98312 | tf_op jit(solution)/shard_map/ppermute | solution.py:14
  186.1 1.2 collective-permute-start.2
Sparse Core Ops, SparseCore 0:
  158.1 23.3 reduce-scatter.3
Sparse Core Ops, SparseCore 1:
  177.0 131.7 all-gather.2
